TPU v7x, 32 devices: a whole 2x2x4 slice. The times are simulated.
32 devices in a mesh: cuts: 2 (over x), mode: 16 (over z, y, core).
Axes of the slice: x: 2, y: 2, z: 4, core: 2. Of those that a mesh axis runs over, the one named last changes fastest.
Arguments:
- stem_tensor: float32 [2, 2, 16, 512, 512], P(None, 'cuts', 'mode'), parts along dimension 1, may hold values from -6 to 6
- branch_tensors: float32 [4, 2, 512, 512], replicated, may hold values from -0.1875 to 0.1875
- branch_order: int32 [4], replicated, may hold values from 0 to 3, each once
Outputs:
- new_stem: float32 [2, 2, 16, 512, 512], P(None, 'cuts', 'mode'), parts along dimension 1
There are 2 independent parts, one for each index of `cuts`. A program takes and returns all parts, laid end to end along the dimension named above; an argument that names none is the same for every part. Nothing has to cross between parts.
Inputs may be any that keep to these rules, and one draw needn't show every extreme that they name: `branch_order`: a permutation of the 4 branch tensors.
All inputs are finite; a program needn't handle non-finite values.
Results may differ from a plain program's by a relative error of at most 0.00007.
Values sent between devices are 32-bit elements; how exact they have to be, the bound alone decides.
A program may use at most 64 MiB of HBM per device.

v0:
```python
import jax
import jax.numpy as jnp
from jax import lax
from jax.sharding import PartitionSpec as P


def complex_product(first, second, form):
    high = lax.Precision.HIGHEST
    real = jnp.einsum(form, first[0], second[0], precision=high) - jnp.einsum(
        form, first[1], second[1], precision=high
    )
    imag = jnp.einsum(form, first[0], second[1], precision=high) + jnp.einsum(
        form, first[1], second[0], precision=high
    )
    return jnp.stack([real, imag])


def on_device(stem_tensor, branch_tensors, branch_order):
    field = stem_tensor[:, :, 0]
    chosen = [branch_tensors[branch_order[index]] for index in range(4)]
    field = complex_product(field, chosen[0], "sce,cd->sde")
    field = complex_product(field, chosen[1], "sce,ed->scd")
    moved = lax.all_to_all(field[:, :, None], "mode", split_axis=3, concat_axis=2, tiled=True)
    merged = moved.reshape(field.shape)
    merged = complex_product(merged, chosen[2], "sce,cd->sde")
    return complex_product(merged, chosen[3], "sce,ed->scd")[:, :, None]


def solution(mesh):
    return jax.shard_map(
        on_device,
        mesh=mesh,
        in_specs=(P(None, "cuts", "mode", None, None), P(), P()),
        out_specs=P(None, "cuts", "mode", None, None),
        check_vma=False,
    )
```

profile of v0, /device:TPU:13, one launch (start us, length us, event | category | flops | bytes accessed | tf_op | source)
XLA Modules:
  0.0 113.0 jit_solution(4636353543271433322)
XLA Ops:
  0.0 1.5 %fusion.45 = (s32[1]{0:T(128)}, s32[1]{0:T(128)}, s32[1]{0:T(128)}, s32[1]{0:T(128)}) fusion(s32[4]{0:T(128)} %param.5), kind=kLoop, calls=%fused_computation.63 | loop fusion | bytes 32 | tf_op jit(solution)/shard_map/slice | solution.py:20
  4.7 0.0 copy-start
  4.7 3.5 %fusion.14 = f32[512,512]{1,0:T(8,128)S(1)} fusion(f32[2,1,1,512,512]{4,3,2,1,0:T(8,128)} %param.3, f32[4,2,512,512]{3,2,1,0:T(8,128)} %param.4, s32[]{:T(128)S(6)} %select_n.13), kind=kOutput, calls=%fused_computation.32 | convolution fusion | flops 1610612736 | bytes 3145732 | tf_op jit(solution)/shard_map/sce,cd->sde/dot_general | solution.py:9
  8.2 4.4 %fusion.12 = f32[512,512]{1,0:T(8,128)} fusion(f32[2,1,1,512,512]{4,3,2,1,0:T(8,128)} %param.3, f32[4,2,512,512]{3,2,1,0:T(8,128)} %param.4, s32[]{:T(128)S(6)} %select_n.13, s32[]{:T(128)S(6)} %add.36), kind=kOutput, calls=%fused_computation.30 | convolution fusion | flops 1610612736 | bytes 3145736 | tf_op jit(solution)/shard_map/sce,cd->sde/dot_general | solution.py:12
  12.6 3.4 %convolution_subtract_fusion.3 = f32[512,512]{1,0:T(8,128)S(1)} fusion(f32[512,512]{1,0:T(8,128)S(1)} %fusion.14, f32[2,1,1,512,512]{4,3,2,1,0:T(8,128)} %param.3, f32[4,2,512,512]{3,2,1,0:T(8,128)} %param.4, s32[]{:T(128)S(6)} %select_n.13, s32[]{:T(128)S(6)} %add.36), kind=kOutput, calls=%fused_computation.13 | convolution fusion | flops 1610874880 | bytes 4194312 | tf_op jit(solution)/shard_map/sce,cd->sde/dot_general | solution.py:9
  16.6 3.1 %fusion.26 = f32[512,512]{1,0:T(8,128)S(1)} fusion(f32[512,512]{1,0:T(8,128)S(1)} %convolution_subtract_fusion.3, f32[4,2,512,512]{3,2,1,0:T(8,128)} %param.4, s32[]{:T(128)S(6)} %select_n.14, s32[]{:T(128)S(6)} %add.36), kind=kOutput, calls=%fused_computation.44 | convolution fusion | flops 1610612736 | bytes 3145736 | tf_op jit(solution)/shard_map/sce,ed->scd/dot_general | solution.py:12
  19.7 3.1 %fusion.24 = f32[512,512]{1,0:T(8,128)S(1)} fusion(f32[512,512]{1,0:T(8,128)S(1)} %convolution_subtract_fusion.3, f32[4,2,512,512]{3,2,1,0:T(8,128)} %param.4, s32[]{:T(128)S(6)} %select_n.14), kind=kOutput, calls=%fused_computation.42 | convolution fusion | flops 1610612736 | bytes 3145732 | tf_op jit(solution)/shard_map/sce,ed->scd/dot_general | solution.py:9
  22.8 0.0 copy-done
  22.8 3.4 %convolution_add_fusion.3 = f32[512,512]{1,0:T(8,128)S(1)} fusion(f32[512,512]{1,0:T(8,128)} %fusion.12, f32[2,1,1,512,512]{4,3,2,1,0:T(8,128)S(1)} %copy-done, f32[4,2,512,512]{3,2,1,0:T(8,128)} %param.4, s32[]{:T(128)S(6)} %select_n.13), kind=kOutput, calls=%fused_computation.12 | convolution fusion | flops 1610874880 | bytes 4194308 | tf_op jit(solution)/shard_map/sce,cd->sde/dot_general | solution.py:12
  26.2 3.3 %fusion.3 = f32[1,1,512,512]{3,2,1,0:T(8,128)S(1)} fusion(f32[512,512]{1,0:T(8,128)S(1)} %fusion.24, f32[512,512]{1,0:T(8,128)S(1)} %convolution_add_fusion.3, f32[4,2,512,512]{3,2,1,0:T(8,128)} %param.4, s32[]{:T(128)S(6)} %select_n.14, s32[]{:T(128)S(6)} %add.36), kind=kOutput, calls=%fused_computation.11 | convolution fusion | flops 1610874880 | bytes 4194312 | tf_op jit(solution)/shard_map/sce,ed->scd/dot_general | solution.py:9
  29.5 3.1 %fusion.2 = f32[1,1,512,512]{3,2,1,0:T(8,128)S(1)} fusion(f32[512,512]{1,0:T(8,128)S(1)} %fusion.26, f32[512,512]{1,0:T(8,128)S(1)} %convolution_add_fusion.3, f32[4,2,512,512]{3,2,1,0:T(8,128)} %param.4, s32[]{:T(128)S(6)} %select_n.14), kind=kOutput, calls=%fused_computation.9 | convolution fusion | flops 1610874880 | bytes 4194308 | tf_op jit(solution)/shard_map/sce,ed->scd/dot_general | solution.py:12
  32.6 0.2 maximum_bitcast_fusion
  32.7 2.9 %copy.5 = f32[2,1,1,512,512]{4,0,2,1,3:T(2,128)} copy(f32[2,1,1,512,512]{4,3,0,2,1:T(8,128)S(1)} %maximum_bitcast_fusion) | data formatting | bytes 4194304 | tf_op jit(solution)/shard_map/broadcast_in_dim | solution.py:23
  35.7 6.5 %all-to-all-start = ((f32[2,1,1,512,512]{4,0,2,1,3:T(2,128)}), f32[2,1,1,512,512]{4,0,2,1,3:T(2,128)S(1)}, u32[]{:S(2)}, u32[]{:S(2)}) async-start(f32[2,1,1,512,512]{4,0,2,1,3:T(2,128)} %copy.5), calls=%async_computation | async-start | bytes 4194304 | tf_op jit(solution)/shard_map/all_to_all | solution.py:23
  46.1 43.5 %all-to-all-done = f32[2,1,1,512,512]{4,0,2,1,3:T(2,128)S(1)} async-done(((f32[2,1,1,512,512]{4,0,2,1,3:T(2,128)}), f32[2,1,1,512,512]{4,0,2,1,3:T(2,128)S(1)}, u32[]{:S(2)}, u32[]{:S(2)}) %all-to-all-start) | async-done | bytes 2097184 | tf_op jit(solution)/shard_map/all_to_all | solution.py:23
  89.6 0.0 slice-start
  89.6 1.6 %fusion.44 = (f32[1,1,1,512,512]{4,0,2,1,3:T(1,128)S(1)}, f32[1,1,1,512,512]{4,0,2,1,3:T(1,128)S(1)}) fusion(f32[2,1,1,512,512]{4,0,2,1,3:T(2,128)S(1)} %all-to-all-done), kind=kLoop, calls=%fused_computation.62 | loop fusion | bytes 4194304 | tf_op jit(solution)/shard_map/slice | solution.py:10
  91.2 3.1 %fusion.6 = f32[512,512]{1,0:T(8,128)S(1)} fusion(f32[1,1,1,512,512]{4,0,2,1,3:T(1,128)S(1)} %get-tuple-element.6, f32[4,2,512,512]{3,2,1,0:T(8,128)} %param.4, s32[]{:T(128)S(6)} %select_n.12, s32[]{:T(128)S(6)} %add.36), kind=kOutput, calls=%fused_computation.24 | convolution fusion | flops 1610612736 | bytes 3145736 | tf_op jit(solution)/shard_map/sce,cd->sde/dot_general | solution.py:12
  94.3 0.0 slice-start.1
  94.3 3.2 %fusion.8 = f32[512,512]{1,0:T(8,128)S(1)} fusion(f32[1,1,1,512,512]{4,0,2,1,3:T(1,128)S(1)} %get-tuple-element.6, f32[4,2,512,512]{3,2,1,0:T(8,128)} %param.4, s32[]{:T(128)S(6)} %select_n.12), kind=kOutput, calls=%fused_computation.26 | convolution fusion | flops 1610612736 | bytes 3145732 | tf_op jit(solution)/shard_map/sce,cd->sde/dot_general | solution.py:9
  97.6 3.1 %convolution_subtract_fusion.1 = f32[512,512]{1,0:T(8,128)S(1)} fusion(f32[512,512]{1,0:T(8,128)S(1)} %fusion.8, f32[1,1,1,512,512]{4,0,2,1,3:T(1,128)S(1)} %get-tuple-element.5, f32[4,2,512,512]{3,2,1,0:T(8,128)} %param.4, s32[]{:T(128)S(6)} %select_n.12, s32[]{:T(128)S(6)} %add.36), kind=kOutput, calls=%fused_computation.7 | convolution fusion | flops 1610874880 | bytes 4194312 | tf_op jit(solution)/shard_map/sce,cd->sde/dot_general | solution.py:9
  100.7 3.1 %fusion.27 = f32[512,512]{1,0:T(8,128)S(1)} fusion(f32[512,512]{1,0:T(8,128)S(1)} %convolution_subtract_fusion.1, f32[4,2,512,512]{3,2,1,0:T(8,128)} %param.4, s32[]{:T(128)S(6)} %select_n.15, s32[]{:T(128)S(6)} %add.36), kind=kOutput, calls=%fused_computation.45 | convolution fusion | flops 1610612736 | bytes 3145736 | tf_op jit(solution)/shard_map/sce,ed->scd/dot_general | solution.py:12
  103.8 0.0 slice-done
  103.8 0.0 slice-done.1
  103.8 1.8 %fusion.25 = f32[512,512]{1,0:T(8,128)S(1)} fusion(f32[512,512]{1,0:T(8,128)S(1)} %convolution_subtract_fusion.1, f32[4,2,512,512]{3,2,1,0:T(8,128)S(1)} %bitcast.79, s32[]{:T(128)S(6)} %select_n.15), kind=kOutput, calls=%fused_computation.43 | convolution fusion | flops 1610612736 | bytes 3145732 | tf_op jit(solution)/shard_map/sce,ed->scd/dot_general | solution.py:9
  105.6 2.2 %convolution_add_fusion.1 = f32[512,512]{1,0:T(8,128)S(1)} fusion(f32[512,512]{1,0:T(8,128)S(1)} %fusion.6, f32[1,1,1,512,512]{4,0,2,1,3:T(1,128)S(1)} %get-tuple-element.5, f32[4,2,512,512]{3,2,1,0:T(8,128)S(1)} %bitcast.79, s32[]{:T(128)S(6)} %select_n.12), kind=kOutput, calls=%fused_computation.6 | convolution fusion | flops 1610874880 | bytes 4194308 | tf_op jit(solution)/shard_map/sce,cd->sde/dot_general | solution.py:12
  107.8 1.8 %fusion.1 = f32[1,1,512,512]{3,2,1,0:T(8,128)S(1)} fusion(f32[512,512]{1,0:T(8,128)S(1)} %fusion.25, f32[512,512]{1,0:T(8,128)S(1)} %convolution_add_fusion.1, f32[4,2,512,512]{3,2,1,0:T(8,128)S(1)} %bitcast.79, s32[]{:T(128)S(6)} %select_n.15, s32[]{:T(128)S(6)} %add.36), kind=kOutput, calls=%fused_computation.5 | convolution fusion | flops 1610874880 | bytes 4194312 | tf_op jit(solution)/shard_map/sce,ed->scd/dot_general | solution.py:9
  109.7 1.8 %fusion = f32[1,1,512,512]{3,2,1,0:T(8,128)S(1)} fusion(f32[512,512]{1,0:T(8,128)S(1)} %fusion.27, f32[512,512]{1,0:T(8,128)S(1)} %convolution_add_fusion.1, f32[4,2,512,512]{3,2,1,0:T(8,128)S(1)} %bitcast.79, s32[]{:T(128)S(6)} %select_n.15), kind=kOutput, calls=%fused_computation.3 | convolution fusion | flops 1610874880 | bytes 4194308 | tf_op jit(solution)/shard_map/sce,ed->scd/dot_general | solution.py:12
  111.5 1.5 %maximum_bitcast_fusion.1 = f32[2,1,1,512,512]{4,3,2,1,0:T(8,128)} fusion(f32[1,1,512,512]{3,2,1,0:T(8,128)S(1)} %fusion, f32[1,1,512,512]{3,2,1,0:T(8,128)S(1)} %fusion.1), kind=kLoop, calls=%fused_computation.1 | loop fusion | flops 524288 | bytes 4194304 | tf_op jit(solution)/shard_map/broadcast_in_dim | solution.py:26
  (1 shorter events, 0.0 us)
Async XLA Ops:
  4.7 18.1 %copy-start = (f32[2,1,1,512,512]{4,3,2,1,0:T(8,128)S(1)}, f32[2,1,1,512,512]{4,3,2,1,0:T(8,128)}, u32[]{:S(2)}) copy-start(f32[2,1,1,512,512]{4,3,2,1,0:T(8,128)} %param.3) | copy-start | bytes 6291460
  35.7 53.9 %all-to-all-start = ((f32[2,1,1,512,512]{4,0,2,1,3:T(2,128)}), f32[2,1,1,512,512]{4,0,2,1,3:T(2,128)S(1)}, u32[]{:S(2)}, u32[]{:S(2)}) async-start(f32[2,1,1,512,512]{4,0,2,1,3:T(2,128)} %copy.5), calls=%async_computation | async-start | bytes 4194304 | tf_op jit(solution)/shard_map/all_to_all | solution.py:23
  89.6 14.2 %slice-start = ((s8[8388608]{0:T(1024)(128)(4,1)}), s8[4194304]{0:T(1024)(128)(4,1)S(1)}, s32[]{:S(2)}) async-start(s8[8388608]{0:T(1024)(128)(4,1)} %bitcast.78), calls=%async_computation.1 | async-start | bytes 8388608
  94.3 9.4 %slice-start.1 = ((s8[8388608]{0:T(1024)(128)(4,1)}), s8[4194304]{0:T(1024)(128)(4,1)S(1)}, s32[]{:S(2)}) async-start(s8[8388608]{0:T(1024)(128)(4,1)} %bitcast.78), calls=%async_computation.2 | async-start | bytes 8388608
where the time goes:
time: 114 us; the launch traced here: 113 us
  matrix products  47.3 us (41%)
  waiting for transfers between devices  43.5 us (38%)
  between operations  7.96 us (7%)
  starting transfers between devices  6.52 us (6%)
  local copies, waits for them, and re-layouts  6.03 us (5%)
  other arithmetic  1.66 us (1%)
    all_to_all x1, waiting for transfers between devices, on_device(): lax.all_to_all(field[:, :, None], 'mode', split_axis=3, concat_axis=2, ti...  43.5 us
    dot_general x4, matrix products, complex_product(): jnp.einsum(form, first[0], second[1], precision=high)  13.6 us
    dot_general x4, matrix products, complex_product(): jnp.einsum(form, first[0], second[0], precision=high)  11.7 us
    dot_general x4, matrix products, complex_product(): jnp.einsum(form, first[1], second[1], precision=high)  11.6 us
    dot_general x4, matrix products, complex_product(): jnp.einsum(form, first[1], second[0], precision=high)  10.5 us
    all_to_all x1, starting transfers between devices, on_device(): lax.all_to_all(field[:, :, None], 'mode', split_axis=3, concat_axis=2, ti...  6.52 us
    broadcast_in_dim x1, local copies, waits for them, and re-layouts, on_device(): field[:, :, None]  2.94 us
  transfers between devices with their start and end apart: 1, of which 1 were waited for; matrix products, arithmetic and copies ran while one was open for 0% of the time, Pallas kernels for 0%

commit v1 on v0

--- a/solution.py
+++ b/solution.py
@@ -20,7 +20,12 @@
     chosen = [branch_tensors[branch_order[index]] for index in range(4)]
     field = complex_product(field, chosen[0], "sce,cd->sde")
     field = complex_product(field, chosen[1], "sce,ed->scd")
-    moved = lax.all_to_all(field[:, :, None], "mode", split_axis=3, concat_axis=2, tiled=True)
+    moved = jnp.concatenate(
+        lax.all_to_all(
+            jnp.stack(jnp.split(field[:, :, None], lax.axis_size("mode"), axis=3)), "mode", 0, 0
+        ),
+        axis=2,
+    )
     merged = moved.reshape(field.shape)
     merged = complex_product(merged, chosen[2], "sce,cd->sde")
     return complex_product(merged, chosen[3], "sce,ed->scd")[:, :, None]

time: 114 us -> 119 us (1.044)
  local copies, waits for them, and re-layouts: 6.03 us -> 12.4 us
    unnamed x6 -> x23, local copies, waits for them, and re-layouts: 0.02 us -> 9.98 us
    broadcast_in_dim x1 -> x0, local copies, waits for them, and re-layouts: 2.94 us -> none  [on_device(): field[:, :, None]]
    slice x1, local copies, waits for them, and re-layouts: 1.62 us -> 0.26 us  [complex_product(): first[1]]
where the time goes in v1:
time: 119 us; the launch traced here: 118 us
  matrix products  46.4 us (39%)
  waiting for transfers between devices  43.6 us (37%)
  local copies, waits for them, and re-layouts  12.4 us (10%)
  between operations  7.8 us (7%)
  starting transfers between devices  6.52 us (5%)
  other arithmetic  1.66 us (1%)
    all_to_all x1, waiting for transfers between devices, on_device(): lax.all_to_all(jnp.stack(jnp.split(field[:, :, None], lax.axis_size('mode...  43.6 us
    dot_general x4, matrix products, complex_product(): jnp.einsum(form, first[0], second[1], precision=high)  13.4 us
    dot_general x4, matrix products, complex_product(): jnp.einsum(form, first[0], second[0], precision=high)  11.6 us
    dot_general x4, matrix products, complex_product(): jnp.einsum(form, first[1], second[1], precision=high)  11.5 us
    unnamed x23, local copies, waits for them, and re-layouts  9.98 us
    dot_general x4, matrix products, complex_product(): jnp.einsum(form, first[1], second[0], precision=high)  9.86 us
    all_to_all x1, starting transfers between devices, on_device(): lax.all_to_all(jnp.stack(jnp.split(field[:, :, None], lax.axis_size('mode...  6.52 us
  transfers between devices with their start and end apart: 1, of which 1 were waited for; matrix products, arithmetic and copies ran while one was open for 0% of the time, Pallas kernels for 0%

profile of v1, /device:TPU:13, one launch (start us, length us, event | category | flops | bytes accessed | tf_op | source)
XLA Modules:
  0.0 118.4 jit_solution(4246238176071900797)
XLA Ops:
  0.0 0.0 copy-start
  0.0 1.5 %fusion.53 = (s32[1]{0:T(128)}, s32[1]{0:T(128)}, s32[1]{0:T(128)}, s32[1]{0:T(128)}) fusion(s32[4]{0:T(128)} %param.5), kind=kLoop, calls=%fused_computation.87 | loop fusion | bytes 32 | tf_op jit(solution)/shard_map/slice | solution.py:20
  4.7 3.4 %fusion.8 = f32[512,512]{1,0:T(8,128)S(1)} fusion(f32[2,1,1,512,512]{4,3,2,1,0:T(8,128)} %param.3, f32[4,2,512,512]{3,2,1,0:T(8,128)} %param.4, s32[]{:T(128)S(6)} %select_n.13), kind=kOutput, calls=%fused_computation.26 | convolution fusion | flops 1610612736 | bytes 3145732 | tf_op jit(solution)/shard_map/sce,cd->sde/dot_general | solution.py:9
  8.1 0.0 copy-done
  8.1 4.1 %fusion.6 = f32[512,512]{1,0:T(8,128)} fusion(f32[2,1,1,512,512]{4,3,2,1,0:T(8,128)S(1)} %copy-done, f32[4,2,512,512]{3,2,1,0:T(8,128)} %param.4, s32[]{:T(128)S(6)} %select_n.13, s32[]{:T(128)S(6)} %add.36), kind=kOutput, calls=%fused_computation.24 | convolution fusion | flops 1610612736 | bytes 3145736 | tf_op jit(solution)/shard_map/sce,cd->sde/dot_general | solution.py:12
  12.2 3.1 %convolution_subtract_fusion.3 = f32[512,512]{1,0:T(8,128)S(1)} fusion(f32[512,512]{1,0:T(8,128)S(1)} %fusion.8, f32[2,1,1,512,512]{4,3,2,1,0:T(8,128)S(1)} %copy-done, f32[4,2,512,512]{3,2,1,0:T(8,128)} %param.4, s32[]{:T(128)S(6)} %select_n.13, s32[]{:T(128)S(6)} %add.36), kind=kOutput, calls=%fused_computation.13 | convolution fusion | flops 1610874880 | bytes 4194312 | tf_op jit(solution)/shard_map/sce,cd->sde/dot_general | solution.py:9
  15.9 3.1 %fusion.17 = f32[512,512]{1,0:T(8,128)S(1)} fusion(f32[512,512]{1,0:T(8,128)S(1)} %convolution_subtract_fusion.3, f32[4,2,512,512]{3,2,1,0:T(8,128)} %param.4, s32[]{:T(128)S(6)} %select_n.14, s32[]{:T(128)S(6)} %add.36), kind=kOutput, calls=%fused_computation.35 | convolution fusion | flops 1610612736 | bytes 3145736 | tf_op jit(solution)/shard_map/sce,ed->scd/dot_general | solution.py:12
  18.9 0.0 copy-start.1
  19.0 3.2 %fusion.15 = f32[512,512]{1,0:T(8,128)S(1)} fusion(f32[512,512]{1,0:T(8,128)S(1)} %convolution_subtract_fusion.3, f32[4,2,512,512]{3,2,1,0:T(8,128)} %param.4, s32[]{:T(128)S(6)} %select_n.14), kind=kOutput, calls=%fused_computation.33 | convolution fusion | flops 1610612736 | bytes 3145732 | tf_op jit(solution)/shard_map/sce,ed->scd/dot_general | solution.py:9
  22.1 0.0 copy-done.1
  22.1 3.1 %convolution_add_fusion.3 = f32[512,512]{1,0:T(8,128)S(1)} fusion(f32[512,512]{1,0:T(8,128)S(1)} %copy-done.1, f32[2,1,1,512,512]{4,3,2,1,0:T(8,128)S(1)} %copy-done, f32[4,2,512,512]{3,2,1,0:T(8,128)} %param.4, s32[]{:T(128)S(6)} %select_n.13), kind=kOutput, calls=%fused_computation.12 | convolution fusion | flops 1610874880 | bytes 4194308 | tf_op jit(solution)/shard_map/sce,cd->sde/dot_general | solution.py:12
  25.2 3.3 %fusion.3 = f32[1,1,512,512]{3,2,1,0:T(8,128)S(1)} fusion(f32[512,512]{1,0:T(8,128)S(1)} %fusion.15, f32[512,512]{1,0:T(8,128)S(1)} %convolution_add_fusion.3, f32[4,2,512,512]{3,2,1,0:T(8,128)} %param.4, s32[]{:T(128)S(6)} %select_n.14, s32[]{:T(128)S(6)} %add.36), kind=kOutput, calls=%fused_computation.11 | convolution fusion | flops 1610874880 | bytes 4194312 | tf_op jit(solution)/shard_map/sce,ed->scd/dot_general | solution.py:9
  28.5 3.1 %fusion.2 = f32[1,1,512,512]{3,2,1,0:T(8,128)S(1)} fusion(f32[512,512]{1,0:T(8,128)S(1)} %fusion.17, f32[512,512]{1,0:T(8,128)S(1)} %convolution_add_fusion.3, f32[4,2,512,512]{3,2,1,0:T(8,128)} %param.4, s32[]{:T(128)S(6)} %select_n.14), kind=kOutput, calls=%fused_computation.9 | convolution fusion | flops 1610874880 | bytes 4194308 | tf_op jit(solution)/shard_map/sce,ed->scd/dot_general | solution.py:12
  31.6 0.2 maximum_bitcast_fusion
  31.8 0.7 fusion.35
  32.4 0.7 fusion.34
  33.1 0.7 fusion.33
  33.8 0.7 fusion.32
  34.4 0.7 fusion.31
  35.1 0.7 fusion.30
  35.7 0.7 fusion.29
  36.4 0.7 fusion.28
  37.1 0.7 fusion.27
  37.7 0.7 fusion.26
  38.4 0.7 fusion.25
  39.1 0.7 fusion.24
  39.7 0.7 fusion.23
  40.4 0.7 fusion.22
  41.1 0.7 fusion.21
  41.7 0.7 fusion.20
  42.4 6.5 %all-to-all-start = ((f32[16,2,1,1,32,512]{5,4,1,3,2,0:T(8,128)}), f32[16,2,1,1,32,512]{5,4,1,3,2,0:T(8,128)S(1)}, u32[]{:S(2)}, u32[]{:S(2)}) async-start(f32[16,2,1,1,32,512]{5,4,1,3,2,0:T(8,128)} %fusion.20), calls=%async_computation | async-start | bytes 4194304 | tf_op jit(solution)/shard_map/all_to_all | solution.py:24
  52.7 43.6 %all-to-all-done = f32[16,2,1,1,32,512]{5,4,1,3,2,0:T(8,128)S(1)} async-done(((f32[16,2,1,1,32,512]{5,4,1,3,2,0:T(8,128)}), f32[16,2,1,1,32,512]{5,4,1,3,2,0:T(8,128)S(1)}, u32[]{:S(2)}, u32[]{:S(2)}) %all-to-all-start) | async-done | bytes 2097184 | tf_op jit(solution)/shard_map/all_to_all | solution.py:24
  96.3 0.0 slice-start
  96.3 0.3 fusion.52
  96.6 3.2 %fusion.18 = f32[512,512]{1,0:T(8,128)S(1)} fusion(f32[512,512]{1,0:T(8,128)S(1)} %bitcast.143, f32[4,2,512,512]{3,2,1,0:T(8,128)} %param.4, s32[]{:T(128)S(6)} %select_n.12, s32[]{:T(128)S(6)} %add.36), kind=kOutput, calls=%fused_computation.36 | convolution fusion | flops 1610612736 | bytes 3145736 | tf_op jit(solution)/shard_map/sce,cd->sde/dot_general | solution.py:12
  99.8 0.0 slice-start.1
  99.9 3.2 %fusion.14 = f32[512,512]{1,0:T(8,128)S(1)} fusion(f32[512,512]{1,0:T(8,128)S(1)} %bitcast.144, f32[4,2,512,512]{3,2,1,0:T(8,128)} %param.4, s32[]{:T(128)S(6)} %select_n.12), kind=kOutput, calls=%fused_computation.32 | convolution fusion | flops 1610612736 | bytes 3145732 | tf_op jit(solution)/shard_map/sce,cd->sde/dot_general | solution.py:9
  103.1 3.1 %convolution_subtract_fusion.1 = f32[512,512]{1,0:T(8,128)S(1)} fusion(f32[512,512]{1,0:T(8,128)S(1)} %fusion.14, f32[512,512]{1,0:T(8,128)S(1)} %bitcast.141, f32[4,2,512,512]{3,2,1,0:T(8,128)} %param.4, s32[]{:T(128)S(6)} %select_n.12, s32[]{:T(128)S(6)} %add.36), kind=kOutput, calls=%fused_computation.7 | convolution fusion | flops 1610874880 | bytes 4194312 | tf_op jit(solution)/shard_map/sce,cd->sde/dot_general | solution.py:9
  106.2 3.1 %fusion.19 = f32[512,512]{1,0:T(8,128)S(1)} fusion(f32[512,512]{1,0:T(8,128)S(1)} %convolution_subtract_fusion.1, f32[4,2,512,512]{3,2,1,0:T(8,128)} %param.4, s32[]{:T(128)S(6)} %select_n.15, s32[]{:T(128)S(6)} %add.36), kind=kOutput, calls=%fused_computation.37 | convolution fusion | flops 1610612736 | bytes 3145736 | tf_op jit(solution)/shard_map/sce,ed->scd/dot_general | solution.py:12
  109.3 0.0 slice-done
  109.3 0.0 slice-done.1
  109.3 1.8 %fusion.16 = f32[512,512]{1,0:T(8,128)S(1)} fusion(f32[512,512]{1,0:T(8,128)S(1)} %convolution_subtract_fusion.1, f32[4,2,512,512]{3,2,1,0:T(8,128)S(1)} %bitcast.140, s32[]{:T(128)S(6)} %select_n.15), kind=kOutput, calls=%fused_computation.34 | convolution fusion | flops 1610612736 | bytes 3145732 | tf_op jit(solution)/shard_map/sce,ed->scd/dot_general | solution.py:9
  111.1 1.9 %convolution_add_fusion.1 = f32[512,512]{1,0:T(8,128)S(1)} fusion(f32[512,512]{1,0:T(8,128)S(1)} %fusion.18, f32[512,512]{1,0:T(8,128)S(1)} %bitcast.142, f32[4,2,512,512]{3,2,1,0:T(8,128)S(1)} %bitcast.140, s32[]{:T(128)S(6)} %select_n.12), kind=kOutput, calls=%fused_computation.6 | convolution fusion | flops 1610874880 | bytes 4194308 | tf_op jit(solution)/shard_map/sce,cd->sde/dot_general | solution.py:12
  113.0 2.1 %fusion.1 = f32[1,1,512,512]{3,2,1,0:T(8,128)S(1)} fusion(f32[512,512]{1,0:T(8,128)S(1)} %fusion.16, f32[512,512]{1,0:T(8,128)S(1)} %convolution_add_fusion.1, f32[4,2,512,512]{3,2,1,0:T(8,128)S(1)} %bitcast.140, s32[]{:T(128)S(6)} %select_n.15, s32[]{:T(128)S(6)} %add.36), kind=kOutput, calls=%fused_computation.5 | convolution fusion | flops 1610874880 | bytes 4194312 | tf_op jit(solution)/shard_map/sce,ed->scd/dot_general | solution.py:9
  115.1 1.8 %fusion = f32[1,1,512,512]{3,2,1,0:T(8,128)S(1)} fusion(f32[512,512]{1,0:T(8,128)S(1)} %fusion.19, f32[512,512]{1,0:T(8,128)S(1)} %convolution_add_fusion.1, f32[4,2,512,512]{3,2,1,0:T(8,128)S(1)} %bitcast.140, s32[]{:T(128)S(6)} %select_n.15), kind=kOutput, calls=%fused_computation.3 | convolution fusion | flops 1610874880 | bytes 4194308 | tf_op jit(solution)/shard_map/sce,ed->scd/dot_general | solution.py:12
  117.0 1.5 %maximum_bitcast_fusion.1 = f32[2,1,1,512,512]{4,3,2,1,0:T(8,128)} fusion(f32[1,1,512,512]{3,2,1,0:T(8,128)S(1)} %fusion, f32[1,1,512,512]{3,2,1,0:T(8,128)S(1)} %fusion.1), kind=kLoop, calls=%fused_computation.1 | loop fusion | flops 524288 | bytes 4194304 | tf_op jit(solution)/shard_map/broadcast_in_dim | solution.py:31
  (1 shorter events, 0.0 us)
Async XLA Ops:
  0.0 8.1 %copy-start = (f32[2,1,1,512,512]{4,3,2,1,0:T(8,128)S(1)}, f32[2,1,1,512,512]{4,3,2,1,0:T(8,128)}, u32[]{:S(2)}) copy-start(f32[2,1,1,512,512]{4,3,2,1,0:T(8,128)} %param.3) | copy-start | bytes 6291460
  18.9 3.2 %copy-start.1 = (f32[512,512]{1,0:T(8,128)S(1)}, f32[512,512]{1,0:T(8,128)}, u32[]{:S(2)}) copy-start(f32[512,512]{1,0:T(8,128)} %fusion.6) | copy-start | bytes 3145732
  42.4 53.9 %all-to-all-start = ((f32[16,2,1,1,32,512]{5,4,1,3,2,0:T(8,128)}), f32[16,2,1,1,32,512]{5,4,1,3,2,0:T(8,128)S(1)}, u32[]{:S(2)}, u32[]{:S(2)}) async-start(f32[16,2,1,1,32,512]{5,4,1,3,2,0:T(8,128)} %fusion.20), calls=%async_computation | async-start | bytes 4194304 | tf_op jit(solution)/shard_map/all_to_all | solution.py:24
  96.3 12.9 %slice-start = ((s8[8388608]{0:T(1024)(128)(4,1)}), s8[4194304]{0:T(1024)(128)(4,1)S(1)}, s32[]{:S(2)}) async-start(s8[8388608]{0:T(1024)(128)(4,1)} %bitcast.139), calls=%async_computation.1 | async-start | bytes 8388608
  99.8 9.4 %slice-start.1 = ((s8[8388608]{0:T(1024)(128)(4,1)}), s8[4194304]{0:T(1024)(128)(4,1)S(1)}, s32[]{:S(2)}) async-start(s8[8388608]{0:T(1024)(128)(4,1)} %bitcast.139), calls=%async_computation.2 | async-start | bytes 8388608
